TPU v7x, 32 devices: a whole 2x2x4 slice. The times are simulated.
32 devices in a mesh: dp: 4 (over z), ep: 8 (over y, x, core).
Axes of the slice: x: 2, y: 2, z: 4, core: 2. Of those that a mesh axis runs over, the one named last changes fastest.
Arguments:
- tokens: bfloat16 [16384, 1024], P(('dp', 'ep')), may hold values from -6 to 6
- bucket: int32 [32], P(('dp', 'ep')), may hold values from 0 to 1
- expert_ids: int32 [16384, 1], P(('dp', 'ep')), may hold values from 0 to 7
- ln1_gain: float32 [1024], replicated, may hold values from 0.5 to 1.5
- qkv_weight: bfloat16 [1024, 3072], P('ep'), may hold values from -0.1875 to 0.1875
- out_weight: bfloat16 [1024, 1024], P('ep'), may hold values from -0.75 to 0.75
- ln2_gain: float32 [1024], replicated, may hold values from 0.5 to 1.5
- up_weight: bfloat16 [1024, 4096], P('ep'), may hold values from -0.1875 to 0.1875
- down_weight: bfloat16 [4096, 1024], P('ep'), may hold values from -0.1875 to 0.1875
- mix_weight: bfloat16 [1024, 2], replicated, may hold values from -0.1875 to 0.1875
- expert_up: bfloat16 [8, 1024, 4096], P('ep', None, 'dp'), may hold values from -0.1875 to 0.1875
- expert_down: bfloat16 [8, 4096, 1024], P('ep', 'dp'), may hold values from -0.1875 to 0.1875
- cotangent: bfloat16 [16384, 1024], P(('dp', 'ep')), may hold values from -6 to 6
Outputs:
- output: bfloat16 [16384, 1024], P(('dp', 'ep'))
- tokens_grad: float32 [16384, 1024], P(('dp', 'ep'))
- ln1_gain_grad: float32 [1024], replicated
- qkv_weight_grad: float32 [1024, 3072], P('ep')
- out_weight_grad: float32 [1024, 1024], P('ep')
- ln2_gain_grad: float32 [1024], replicated
- up_weight_grad: float32 [1024, 4096], P('ep')
- down_weight_grad: float32 [4096, 1024], P('ep')
- mix_weight_grad: float32 [1024, 2], replicated
- expert_up_grad: float32 [8, 1024, 4096], P('ep', None, 'dp')
- expert_down_grad: float32 [8, 4096, 1024], P('ep', 'dp')
All inputs are finite; a program needn't handle non-finite values.
Results may differ from a plain program's by a relative error of at most 0.02.
Values may be sent and summed in bfloat16 or wider, within the bound.
A program may use at most 320 MiB of HBM per device.

v0:
```python
import jax
import jax.numpy as jnp
from jax import lax
from jax.sharding import PartitionSpec as P

HEAD = 64
SHORT_SEQS = 4


def layer_norm(values_in, gain_vec):
    centred = values_in - jnp.mean(values_in, axis=-1, keepdims=True)
    inverse = lax.rsqrt(jnp.mean(centred * centred, axis=-1, keepdims=True) + 1e-05)
    return centred * inverse * gain_vec


def softmax_last(scores):
    row_peak = jnp.max(scores, axis=-1, keepdims=True)
    weights = jnp.exp(scores - row_peak)
    return weights / jnp.sum(weights, axis=-1, keepdims=True)


def gelu_backward(pre_act, act_grad):
    unused, pullback = jax.vjp(jax.nn.gelu, pre_act)
    return pullback(act_grad)[0]


def head_split(qkv_rows):
    length = qkv_rows.shape[0]
    width = qkv_rows.shape[1] // 3
    shaped = qkv_rows.reshape(length, 3, width // HEAD, HEAD)
    return (shaped[:, 0], shaped[:, 1], shaped[:, 2])


def masked_scores(query_rows, key_rows, allowed):
    scores = jnp.einsum(
        "qhd,khd->hqk", query_rows, key_rows, preferred_element_type=jnp.float32
    ) * HEAD ** (-0.5)
    return jnp.where(allowed[None], scores, -1e30)


def attention_forward(qkv_rows, allowed):
    length = qkv_rows.shape[0]
    query_rows, key_rows, value_rows = head_split(qkv_rows)
    scores = masked_scores(query_rows, key_rows, allowed)
    row_peak = jnp.max(scores, axis=-1, keepdims=True)
    weights = jnp.exp(scores - row_peak)
    totals = jnp.sum(weights, axis=-1, keepdims=True)
    prob_low = (weights / totals).astype(jnp.bfloat16)
    mixed_rows = jnp.einsum(
        "hqk,khd->qhd", prob_low, value_rows, preferred_element_type=jnp.float32
    )
    return (mixed_rows.reshape(length, -1).astype(jnp.bfloat16), row_peak + jnp.log(totals))


def attention_backward(qkv_rows, allowed, log_total, attended_grad):
    length = qkv_rows.shape[0]
    query_rows, key_rows, value_rows = head_split(qkv_rows)
    probs_full = jnp.exp(masked_scores(query_rows, key_rows, allowed) - log_total)
    grad_heads = attended_grad.reshape(query_rows.shape)
    prob_grad = jnp.einsum(
        "qhd,khd->hqk", grad_heads, value_rows, preferred_element_type=jnp.float32
    )
    centre = jnp.sum(probs_full * prob_grad, axis=-1, keepdims=True)
    score_grad = (probs_full * (prob_grad - centre)).astype(jnp.bfloat16)
    factor = HEAD ** (-0.5)
    query_grad = (
        jnp.einsum("hqk,khd->qhd", score_grad, key_rows, preferred_element_type=jnp.float32)
        * factor
    )
    key_grad = (
        jnp.einsum("hqk,qhd->khd", score_grad, query_rows, preferred_element_type=jnp.float32)
        * factor
    )
    value_grad = jnp.einsum(
        "hqk,qhd->khd",
        probs_full.astype(jnp.bfloat16),
        grad_heads,
        preferred_element_type=jnp.float32,
    )
    stacked = jnp.stack([query_grad, key_grad, value_grad], axis=1)
    return stacked.reshape(length, -1).astype(jnp.bfloat16)


def on_device(
    tokens,
    bucket,
    expert_ids,
    ln1_gain,
    qkv_weight,
    out_weight,
    ln2_gain,
    up_weight,
    down_weight,
    mix_weight,
    expert_up,
    expert_down,
    cotangent,
):
    length = tokens.shape[0]
    experts = lax.axis_size("ep") * expert_up.shape[0]
    capacity = 5 * length // (4 * experts)
    qkv_full, out_full, up_full, down_full = (
        lax.all_gather(qkv_weight, "ep", axis=0, tiled=True),
        lax.all_gather(out_weight, "ep", axis=0, tiled=True),
        lax.all_gather(up_weight, "ep", axis=0, tiled=True),
        lax.all_gather(down_weight, "ep", axis=0, tiled=True),
    )
    token_rows = tokens.astype(jnp.float32)
    normed_in = layer_norm(token_rows, ln1_gain).astype(jnp.bfloat16)
    qkv_rows = jnp.dot(normed_in, qkv_full, preferred_element_type=jnp.float32).astype(jnp.bfloat16)
    position = jnp.arange(length, dtype=jnp.int32)
    sequence = jnp.where(bucket[0] == 1, 0, position // (length // SHORT_SEQS))
    allowed = jnp.logical_and(
        sequence[:, None] == sequence[None, :], position[None, :] <= position[:, None]
    )
    attended, log_total = attention_forward(qkv_rows, allowed)
    attn_out = jnp.dot(attended, out_full, preferred_element_type=jnp.float32)
    hidden_res = token_rows + attn_out
    mid_low = layer_norm(hidden_res, ln2_gain).astype(jnp.bfloat16)
    dense_pre = jnp.dot(mid_low, up_full, preferred_element_type=jnp.float32)
    dense_act = jax.nn.gelu(dense_pre).astype(jnp.bfloat16)
    dense_out = jnp.dot(dense_act, down_full, preferred_element_type=jnp.float32)
    mixing = softmax_last(jnp.dot(mid_low, mix_weight, preferred_element_type=jnp.float32))
    chosen = expert_ids[:, 0]
    one_hot = (chosen[:, None] == jnp.arange(experts, dtype=jnp.int32)[None, :]).astype(jnp.int32)
    slot_index = jnp.sum(one_hot * (jnp.cumsum(one_hot, axis=0) - 1), axis=1)
    slot_match = (
        slot_index[:, None, None] == jnp.arange(capacity, dtype=jnp.int32)[None, None, :]
    ).astype(jnp.int32)
    table_flat = (
        (one_hot[:, :, None] * slot_match).reshape(length, experts * capacity).astype(jnp.bfloat16)
    )
    sent_rows = jnp.einsum(
        "tk,td->kd", table_flat, mid_low, preferred_element_type=jnp.float32
    ).astype(jnp.bfloat16)
    arrived = lax.all_to_all(
        sent_rows.reshape(experts, capacity, -1), "ep", split_axis=0, concat_axis=1, tiled=True
    )
    slot_rows = lax.all_gather(arrived, "dp", axis=1, tiled=True)
    expert_pre = jnp.einsum(
        "erd,edf->erf", slot_rows, expert_up, preferred_element_type=jnp.float32
    )
    expert_act = jax.nn.gelu(expert_pre).astype(jnp.bfloat16)
    partial_out = jnp.einsum(
        "erf,efd->erd", expert_act, expert_down, preferred_element_type=jnp.float32
    )
    summed_out = lax.psum_scatter(
        partial_out.astype(jnp.bfloat16), "dp", scatter_dimension=1, tiled=True
    )
    returned = lax.all_to_all(summed_out, "ep", split_axis=1, concat_axis=0, tiled=True)
    expert_out = jnp.dot(
        table_flat, returned.reshape(experts * capacity, -1), preferred_element_type=jnp.float32
    )
    result = hidden_res + mixing[:, 0:1] * dense_out + mixing[:, 1:2] * expert_out
    grad_out = cotangent.astype(jnp.float32)
    mix_grad = jnp.stack(
        [jnp.sum(grad_out * dense_out, axis=-1), jnp.sum(grad_out * expert_out, axis=-1)], axis=-1
    )
    logit_grad = (mixing * (mix_grad - jnp.sum(mixing * mix_grad, axis=-1, keepdims=True))).astype(
        jnp.bfloat16
    )
    mix_weight_grad = jnp.einsum(
        "td,tk->dk", mid_low, logit_grad, preferred_element_type=jnp.float32
    )
    dense_grad = (mixing[:, 0:1] * grad_out).astype(jnp.bfloat16)
    down_weight_grad = jnp.einsum(
        "tf,td->fd", dense_act, dense_grad, preferred_element_type=jnp.float32
    )
    dense_act_grad = jnp.einsum(
        "td,fd->tf", dense_grad, down_full, preferred_element_type=jnp.float32
    )
    dense_pre_grad = gelu_backward(dense_pre, dense_act_grad).astype(jnp.bfloat16)
    up_weight_grad = jnp.einsum(
        "td,tf->df", mid_low, dense_pre_grad, preferred_element_type=jnp.float32
    )
    mid_grad = jnp.einsum("tf,df->td", dense_pre_grad, up_full, preferred_element_type=jnp.float32)
    mid_grad = mid_grad + jnp.einsum(
        "tk,dk->td", logit_grad, mix_weight, preferred_element_type=jnp.float32
    )
    expert_grad = (mixing[:, 1:2] * grad_out).astype(jnp.bfloat16)
    sent_grad = jnp.einsum(
        "tk,td->kd", table_flat, expert_grad, preferred_element_type=jnp.float32
    ).astype(jnp.bfloat16)
    arrived_grad = lax.all_to_all(
        sent_grad.reshape(experts, capacity, -1), "ep", split_axis=0, concat_axis=1, tiled=True
    )
    slot_grad = lax.all_gather(arrived_grad, "dp", axis=1, tiled=True)
    expert_act_grad = jnp.einsum(
        "erd,efd->erf", slot_grad, expert_down, preferred_element_type=jnp.float32
    )
    expert_pre_grad = gelu_backward(expert_pre, expert_act_grad).astype(jnp.bfloat16)
    expert_down_grad = jnp.einsum(
        "erf,erd->efd", expert_act, slot_grad, preferred_element_type=jnp.float32
    )
    expert_up_grad = jnp.einsum(
        "erd,erf->edf", slot_rows, expert_pre_grad, preferred_element_type=jnp.float32
    )
    partial_in = jnp.einsum(
        "erf,edf->erd", expert_pre_grad, expert_up, preferred_element_type=jnp.float32
    )
    summed_in = lax.psum_scatter(
        partial_in.astype(jnp.bfloat16), "dp", scatter_dimension=1, tiled=True
    )
    back_rows = lax.all_to_all(summed_in, "ep", split_axis=1, concat_axis=0, tiled=True)
    mid_grad = mid_grad + jnp.dot(
        table_flat, back_rows.reshape(experts * capacity, -1), preferred_element_type=jnp.float32
    )
    unused_mid, mid_pull = jax.vjp(layer_norm, hidden_res, ln2_gain)
    res_part, ln2_gain_grad = mid_pull(mid_grad)
    res_grad = grad_out + res_part
    attn_out_grad = res_grad.astype(jnp.bfloat16)
    out_weight_grad = jnp.einsum(
        "td,te->de", attended, attn_out_grad, preferred_element_type=jnp.float32
    )
    attended_grad = jnp.einsum(
        "te,de->td", attn_out_grad, out_full, preferred_element_type=jnp.float32
    ).astype(jnp.bfloat16)
    qkv_grad = attention_backward(qkv_rows, allowed, log_total, attended_grad)
    qkv_weight_grad = jnp.einsum(
        "td,tk->dk", normed_in, qkv_grad, preferred_element_type=jnp.float32
    )
    normed_grad = jnp.einsum("tk,dk->td", qkv_grad, qkv_full, preferred_element_type=jnp.float32)
    unused_in, in_pull = jax.vjp(layer_norm, token_rows, ln1_gain)
    token_part, ln1_gain_grad = in_pull(normed_grad)
    tokens_grad = res_grad + token_part
    batch_sums = (
        lax.psum_scatter(
            qkv_weight_grad.astype(jnp.bfloat16), "ep", scatter_dimension=0, tiled=True
        ).astype(jnp.float32),
        lax.psum_scatter(
            out_weight_grad.astype(jnp.bfloat16), "ep", scatter_dimension=0, tiled=True
        ).astype(jnp.float32),
        lax.psum_scatter(
            up_weight_grad.astype(jnp.bfloat16), "ep", scatter_dimension=0, tiled=True
        ).astype(jnp.float32),
        lax.psum_scatter(
            down_weight_grad.astype(jnp.bfloat16), "ep", scatter_dimension=0, tiled=True
        ).astype(jnp.float32),
    )
    dense_shards = (
        lax.psum(batch_sums[0].astype(jnp.bfloat16), "dp").astype(jnp.float32),
        lax.psum(batch_sums[1].astype(jnp.bfloat16), "dp").astype(jnp.float32),
        lax.psum(batch_sums[2].astype(jnp.bfloat16), "dp").astype(jnp.float32),
        lax.psum(batch_sums[3].astype(jnp.bfloat16), "dp").astype(jnp.float32),
    )
    small_sums = lax.psum((ln1_gain_grad, ln2_gain_grad, mix_weight_grad), ("dp", "ep"))
    return (
        result.astype(jnp.bfloat16),
        tokens_grad,
        small_sums[0],
        dense_shards[0],
        dense_shards[1],
        small_sums[1],
        dense_shards[2],
        dense_shards[3],
        small_sums[2],
        expert_up_grad,
        expert_down_grad,
    )


def solution(mesh):
    placed = (
        P(("dp", "ep"), None),
        P(("dp", "ep")),
        P(("dp", "ep"), None),
        P(),
        P("ep", None),
        P("ep", None),
        P(),
        P("ep", None),
        P("ep", None),
        P(),
        P("ep", None, "dp"),
        P("ep", "dp", None),
        P(("dp", "ep"), None),
    )
    return jax.shard_map(
        on_device,
        mesh=mesh,
        in_specs=placed,
        out_specs=(
            P(("dp", "ep"), None),
            P(("dp", "ep"), None),
            P(),
            P("ep", None),
            P("ep", None),
            P(),
            P("ep", None),
            P("ep", None),
            P(),
            P("ep", None, "dp"),
            P("ep", "dp", None),
        ),
        check_vma=False,
    )
```

profile of v0, /device:TPU:0, one launch (start us, length us, event | category | flops | bytes accessed | tf_op | source)
XLA Modules:
  0.0 1117.8 jit_solution(12316198265122830779)
XLA Ops:
  17.8 40.4 %all-gather.7.cloned.1.call-done = bf16[1024,3072]{1,0:T(8,128)(2,1)} async-done(((bf16[128,3072]{1,0:T(8,128)(2,1)}), bf16[1024,3072]{1,0:T(8,128)(2,1)}) %all-gather.7.cloned.1.call-update) | async-done | bytes 6291472 | tf_op jit(solution)/shard_map/all_gather | solution.py:103
  70.8 10.1 fusion.99
  80.9 8.4 fusion
  89.3 10.1 fusion.56
  105.2 21.3 %all_to_all.42 = bf16[8,80,1024]{2,1,0:T(8,128)(2,1)} all-to-all(bf16[8,80,1024]{2,1,0:T(8,128)(2,1)S(1)} %bitcast.156), channel_id=1, replica_groups=mesh['dp'=4,'ep'=8] {'ep'}, dimensions={0} | all-to-all | bytes 2621440 | tf_op jit(solution)/shard_map/all_to_all | solution.py:136
  126.5 97.3 %all-gather.15.cloned.1.call-done = bf16[1,2560,1024]{2,1,0:T(8,128)(2,1)} async-done(((bf16[1,640,1024]{2,1,0:T(8,128)(2,1)}), bf16[1,2560,1024]{2,1,0:T(8,128)(2,1)}) %all-gather.15.cloned.1.call-update) | async-done | bytes 5242896 | tf_op jit(solution)/shard_map/all_gather | solution.py:139
  223.8 8.6 fusion.28
  246.3 90.7 %reduce-scatter.7.cloned.1.call-done = bf16[1,640,1024]{2,1,0:T(8,128)(2,1)} async-done(((bf16[1,2560,1024]{2,1,0:T(8,128)(2,1)}), bf16[1,640,1024]{2,1,0:T(8,128)(2,1)}) %reduce-scatter.7.cloned.1.call-update) | async-done | bytes 1310736 | tf_op jit(solution)/shard_map/reduce_scatter | solution.py:147
  342.3 10.7 reduce.2
  361.9 41.4 %all-gather.11.cloned.1.call-done = bf16[1024,4096]{1,0:T(8,128)(2,1)} async-done(((bf16[128,4096]{1,0:T(8,128)(2,1)}), bf16[1024,4096]{1,0:T(8,128)(2,1)}) %all-gather.11.cloned.1.call-update) | async-done | bytes 8388624 | tf_op jit(solution)/shard_map/all_gather | solution.py:105
  403.4 10.0 fusion.104
  423.9 35.3 %all-gather.13.cloned.1.call-done = bf16[4096,1024]{1,0:T(8,128)(2,1)} async-done(((bf16[512,1024]{1,0:T(8,128)(2,1)}), bf16[4096,1024]{1,0:T(8,128)(2,1)}) %all-gather.13.cloned.1.call-update) | async-done | bytes 8388624 | tf_op jit(solution)/shard_map/all_gather | solution.py:106
  459.1 13.3 %fusion.49 = (f32[512]{0:T(512)S(1)}, f32[512]{0:T(512)S(1)}, f32[512,1024]{1,0:T(8,128)}) fusion(bf16[512,1024]{1,0:T(8,128)(2,1)} %param.25, f32[512,1024]{1,0:T(8,128)} %fusion.68, bf16[4096,1024]{1,0:T(8,128)(2,1)} %all-gather.13.cloned.1.call-done, f32[512,4096]{1,0:T(8,128)} %fusion.104), kind=kOutput, calls=%fused_computation.71 | convolution fusion | flops 4316462080 | bytes 22024192 | tf_op jit(solution)/shard_map/dot_general | solution.py:122
  473.5 21.3 %all_to_all.43 = bf16[8,80,1024]{2,1,0:T(8,128)(2,1)} all-to-all(bf16[8,80,1024]{2,1,0:T(8,128)(2,1)S(1)} %bitcast.157), channel_id=1, replica_groups=mesh['dp'=4,'ep'=8] {'ep'}, dimensions={0} | all-to-all | bytes 2621440 | tf_op jit(solution)/shard_map/all_to_all | solution.py:184
  495.1 97.0 %all-gather.17.cloned.1.call-done = bf16[1,2560,1024]{2,1,0:T(8,128)(2,1)} async-done(((bf16[1,640,1024]{2,1,0:T(8,128)(2,1)}), bf16[1,2560,1024]{2,1,0:T(8,128)(2,1)}) %all-gather.17.cloned.1.call-update) | async-done | bytes 5242896 | tf_op jit(solution)/shard_map/all_gather | solution.py:187
  592.1 14.9 %fusion.8 = bf16[2560,1024]{1,0:T(8,128)(2,1)S(1)} fusion(f32[2560,1024]{1,0:T(8,128)} %copy-done.41, bf16[1,2560,1024]{2,1,0:T(8,128)(2,1)} %all-gather.17.cloned.1.call-done, bf16[1,1024,1024]{2,1,0:T(8,128)(2,1)S(1)} %copy-done), kind=kOutput, calls=%fused_computation.18 | convolution fusion | flops 5421137920 | bytes 23068672 | tf_op jit(solution)/shard_map/erd,efd->erf/dot_general | solution.py:188
  618.4 10.3 convolution_convert_fusion
  629.0 12.5 %fusion.15 = bf16[512,4096]{1,0:T(8,128)(2,1)S(1)} fusion(f32[512,4096]{1,0:T(8,128)} %fusion.104, bf16[4096,1024]{1,0:T(8,128)(2,1)} %all-gather.13.cloned.1.call-done, bf16[512,1024]{1,0:T(8,128)(2,1)S(1)} %copy-done.13, f32[512]{0:T(512)S(1)} %bitcast.170), kind=kOutput, calls=%fused_computation.26 | convolution fusion | flops 4338483200 | bytes 22022144 | tf_op jit(solution)/shard_map/td,fd->tf/dot_general | solution.py:169
  652.9 56.6 %reduce-scatter.9.cloned.1.call-done = bf16[1,640,1024]{2,1,0:T(8,128)(2,1)} async-done(((bf16[1,2560,1024]{2,1,0:T(8,128)(2,1)}), bf16[1,640,1024]{2,1,0:T(8,128)(2,1)}) %reduce-scatter.9.cloned.1.call-update) | async-done | bytes 1310736 | tf_op jit(solution)/shard_map/reduce_scatter | solution.py:201
  714.4 9.6 reduce.3
  730.3 10.6 fusion.105
  740.9 14.5 %all-to-all-done.3 = bf16[8,2,40960]{2,1,0:T(2,128)(2,1)} async-done(((bf16[8,2,40960]{2,1,0:T(2,128)(2,1)}), bf16[8,2,40960]{2,1,0:T(2,128)(2,1)}, u32[]{:S(2)}, u32[]{:S(2)}) %all-to-all-start.3) | async-done | bytes 1310752 | tf_op jit(solution)/shard_map/all_to_all | solution.py:204
  780.1 11.5 %multiply_reduce_fusion = (f32[16,512]{1,0:T(8,128)S(1)}, f32[16,512,512]{1,2,0:T(8,128)}) fusion(f32[16,512,512]{1,2,0:T(8,128)} %get-tuple-element.32, f32[16,512]{1,0:T(8,128)S(1)} %log_add_fusion, bf16[512,16,64]{0,2,1:T(8,128)(2,1)S(1)} %bitcast.144, bf16[512,3,16,64]{0,3,2,1:T(8,128)(2,1)} %bitcast.139), kind=kOutput, calls=%fused_computation.1 | convolution fusion | flops 549445632 | bytes 35717120 | tf_op jit(solution)/shard_map/qhd,khd->hqk/dot_general | solution.py:60
  791.6 12.9 %multiply_convert_fusion = bf16[16,512,512]{1,2,0:T(8,128)(2,1)S(1)} fusion(f32[16,512,512]{1,2,0:T(8,128)} %get-tuple-element.40, f32[16,512,512]{1,2,0:T(8,128)} %get-tuple-element.32, f32[16,512]{1,0:T(8,128)S(1)} %get-tuple-element.39, f32[16,512]{1,0:T(8,128)S(1)} %log_add_fusion), kind=kLoop, calls=%fused_computation | loop fusion | flops 16777216 | bytes 42008576 | tf_op jit(solution)/shard_map/convert_element_type | solution.py:64
  809.0 9.0 fusion.62
  826.7 10.7 fusion.41
  837.4 28.6 %reduce-scatter.15.cloned.1.call-done = bf16[128,4096]{1,0:T(8,128)(2,1)} async-done(((bf16[1024,4096]{1,0:T(8,128)(2,1)}), bf16[128,4096]{1,0:T(8,128)(2,1)}) %reduce-scatter.15.cloned.1.call-update) | async-done | bytes 1048592 | tf_op jit(solution)/shard_map/reduce_scatter | solution.py:233
  866.0 45.1 %reduce-scatter.13.cloned.1.call-done = bf16[128,1024]{1,0:T(8,128)(2,1)} async-done(((bf16[1024,1024]{1,0:T(8,128)(2,1)}), bf16[128,1024]{1,0:T(8,128)(2,1)}) %reduce-scatter.13.cloned.1.call-update) | async-done | bytes 262160 | tf_op jit(solution)/shard_map/reduce_scatter | solution.py:230
  911.1 65.4 %reduce-scatter.11.cloned.1.call-done = bf16[128,3072]{1,0:T(8,128)(2,1)} async-done(((bf16[1024,3072]{1,0:T(8,128)(2,1)}), bf16[128,3072]{1,0:T(8,128)(2,1)}) %reduce-scatter.11.cloned.1.call-update) | async-done | bytes 786448 | tf_op jit(solution)/shard_map/reduce_scatter | solution.py:227
  976.5 11.6 %fusion.38 = f32[1,1024,1024]{2,1,0:T(8,128)} fusion(bf16[1,2560,1024]{2,1,0:T(8,128)(2,1)} %all-gather.17.cloned.1.call-done, f32[2560,1024]{1,0:T(8,128)} %copy-done.41), kind=kOutput, calls=%fused_computation.64 | convolution fusion | flops 5392302080 | bytes 19922944 | tf_op jit(solution)/shard_map/erf,erd->efd/dot_general | solution.py:192
  996.5 42.8 %all-reduce = (f32[1024]{0:T(1024)}, f32[1024]{0:T(1024)}, f32[1024,2]{0,1:T(2,128)}) all-reduce(f32[1024]{0:T(1024)S(1)} %get-tuple-element.13, f32[1024]{0:T(1024)S(1)} %get-tuple-element.11, f32[1024,2]{0,1:T(2,128)S(1)} %fusion.102), channel_id=1, replica_groups=mesh['dp'=4,'ep'=8] {'dp','ep'}, use_global_device_ids=true, to_apply=%region_22.23 | all-reduce | flops 4096 | bytes 32768 | tf_op jit(solution)/shard_map/psum | solution.py:246
  1043.8 58.4 %all-reduce.4.cloned.1.call-done = (bf16[128,3072]{1,0:T(8,128)(2,1)}, bf16[128,1024]{1,0:T(8,128)(2,1)}, bf16[128,4096]{1,0:T(8,128)(2,1)}, bf16[512,1024]{1,0:T(8,128)(2,1)}) async-done(((bf16[128,3072]{1,0:T(8,128)(2,1)}, bf16[128,1024]{1,0:T(8,128)(2,1)}, bf16[128,4096]{1,0:T(8,128)(2,1)}, bf16[512,1024]{1,0:T(8,128)(2,1)}), (bf16[128,3072]{1,0:T(8,128)(2,1)}, bf16[128,1024]{1,0:T(8,128)(2,1)}, ...) | async-done | bytes 3145744 | tf_op jit(solution)/shard_map/psum | solution.py:241
  (180 shorter events, 161.5 us)
Async XLA Ops:
  7.2 229.2 %copy-start = (bf16[1,1024,1024]{2,1,0:T(8,128)(2,1)S(1)}, bf16[1,1024,1024]{2,1,0:T(8,128)(2,1)}, u32[]{:S(2)}) copy-start(bf16[1,1024,1024]{2,1,0:T(8,128)(2,1)} %param.24) | copy-start | bytes 6291460
  7.2 51.0 %copy-start.5 = (bf16[512,1024]{1,0:T(8,128)(2,1)S(1)}, bf16[512,1024]{1,0:T(8,128)(2,1)}, u32[]{:S(2)}) copy-start(bf16[512,1024]{1,0:T(8,128)(2,1)} %param.13) | copy-start | bytes 3145732
  7.2 51.0 %copy-start.36 = (f32[1024]{0:T(1024)S(1)}, f32[1024]{0:T(1024)}, u32[]{:S(2)}) copy-start(f32[1024]{0:T(1024)} %param.16) | copy-start | bytes 12292
  7.2 51.0 %all-gather.7.cloned.1.call-start = ((), (), s32[]{:S(2)}) async-start(), calls=%async_computation.10 | async-start | bytes 7077888 | tf_op jit(solution)/shard_map/all_gather | solution.py:103
  8.0 91.4 %all-gather.9.cloned.1.call-start = ((), (), s32[]{:S(2)}) async-start(), calls=%async_computation.11 | async-start | bytes 2359296 | tf_op jit(solution)/shard_map/all_gather | solution.py:104
  8.7 215.1 %all-gather.15.cloned.1.call-start = ((), (), s32[]{:S(2)}) async-start(), calls=%async_computation.14 | async-start | bytes 6553600 | tf_op jit(solution)/shard_map/all_gather | solution.py:139
  10.9 55.1 %copy-start.26 = (f32[512]{0:T(512)}, f32[512]{0:T(512)S(1)}, u32[]{:S(2)}) copy-start(f32[512]{0:T(512)S(1)} %broadcast_multiply_fusion.1) | copy-start | bytes 6148
  12.5 53.4 %copy-start.30 = (f32[512]{0:T(512)}, f32[512]{0:T(512)S(1)}, u32[]{:S(2)}) copy-start(f32[512]{0:T(512)S(1)} %fusion.90) | copy-start | bytes 6148
  103.1 23.4 %copy-start.34 = (f32[512]{0:T(512)}, f32[512]{0:T(512)S(1)}, u32[]{:S(2)}) copy-start(f32[512]{0:T(512)S(1)} %multiply_reduce_fusion.3) | copy-start | bytes 6148
  103.1 23.4 %copy-start.28 = (f32[512]{0:T(512)}, f32[512]{0:T(512)S(1)}, u32[]{:S(2)}) copy-start(f32[512]{0:T(512)S(1)} %fusion.91) | copy-start | bytes 6148
  126.5 210.5 %reduce-scatter.7.cloned.1.call-start = ((), (), s32[]{:S(2)}) async-start(), calls=%async_computation.15 | async-start | bytes 6553600 | tf_op jit(solution)/shard_map/reduce_scatter | solution.py:147
  244.7 158.7 %all-gather.11.cloned.1.call-start = ((), (), s32[]{:S(2)}) async-start(), calls=%async_computation.12 | async-start | bytes 9437184 | tf_op jit(solution)/shard_map/all_gather | solution.py:105
  245.3 213.9 %all-gather.13.cloned.1.call-start = ((), (), s32[]{:S(2)}) async-start(), calls=%async_computation.13 | async-start | bytes 9437184 | tf_op jit(solution)/shard_map/all_gather | solution.py:106
  357.4 56.0 %all-to-all-start.1 = ((bf16[8,2,40960]{2,1,0:T(2,128)(2,1)}), bf16[8,2,40960]{2,1,0:T(2,128)(2,1)}, u32[]{:S(2)}, u32[]{:S(2)}) async-start(bf16[8,2,40960]{2,1,0:T(2,128)(2,1)} %reshape.349), calls=%async_computation.2 | async-start | bytes 2621440 | tf_op jit(solution)/shard_map/all_to_all | solution.py:150
  361.7 230.4 %all-gather.17.cloned.1.call-start = ((), (), s32[]{:S(2)}) async-start(), calls=%async_computation.16 | async-start | bytes 6553600 | tf_op jit(solution)/shard_map/all_gather | solution.py:187
  459.1 13.4 %copy-start.11 = (bf16[512,8,80]{0,2,1:T(8,128)(2,1)S(1)}, bf16[512,8,80]{0,2,1:T(8,128)(2,1)}, u32[]{:S(2)}) copy-start(bf16[512,8,80]{0,2,1:T(8,128)(2,1)} %multiply_convert_fusion.6) | copy-start | bytes 1966084
  459.1 13.4 %copy-start.12 = (bf16[512,1024]{1,0:T(8,128)(2,1)S(1)}, bf16[512,1024]{1,0:T(8,128)(2,1)}, u32[]{:S(2)}) copy-start(bf16[512,1024]{1,0:T(8,128)(2,1)} %param.25) | copy-start | bytes 3145732
  494.8 214.6 %reduce-scatter.9.cloned.1.call-start = ((), (), s32[]{:S(2)}) async-start(), calls=%async_computation.17 | async-start | bytes 6553600 | tf_op jit(solution)/shard_map/reduce_scatter | solution.py:201
  592.1 17.3 %copy-start.39 = (bf16[1,1024,1024]{2,1,0:T(8,128)(2,1)S(1)}, bf16[1,1024,1024]{2,1,0:T(8,128)(2,1)}, u32[]{:S(2)}) copy-start(bf16[1,1024,1024]{2,1,0:T(8,128)(2,1)} %param.23) | copy-start | bytes 6291460
  617.2 220.2 %reduce-scatter.17.cloned.1.call-start = ((), (), s32[]{:S(2)}) async-start(), calls=%async_computation.21 | async-start | bytes 9437184 | tf_op jit(solution)/shard_map/reduce_scatter | solution.py:236
  628.7 237.3 %reduce-scatter.15.cloned.1.call-start = ((), (), s32[]{:S(2)}) async-start(), calls=%async_computation.20 | async-start | bytes 9437184 | tf_op jit(solution)/shard_map/reduce_scatter | solution.py:233
  725.8 29.6 %all-to-all-start.3 = ((bf16[8,2,40960]{2,1,0:T(2,128)(2,1)}), bf16[8,2,40960]{2,1,0:T(2,128)(2,1)}, u32[]{:S(2)}, u32[]{:S(2)}) async-start(bf16[8,2,40960]{2,1,0:T(2,128)(2,1)} %reshape.351), calls=%async_computation.5 | async-start | bytes 2621440 | tf_op jit(solution)/shard_map/all_to_all | solution.py:204
  730.1 31.5 %copy-start.23 = (f32[512]{0:T(512)S(1)}, f32[512]{0:T(512)}, u32[]{:S(2)}) copy-start(f32[512]{0:T(512)} %copy-done.22) | copy-start | bytes 6148
  730.1 31.5 %copy-start.25 = (f32[1024]{0:T(1024)S(1)}, f32[1024]{0:T(1024)}, u32[]{:S(2)}) copy-start(f32[1024]{0:T(1024)} %param.19) | copy-start | bytes 12292
  730.1 31.5 %copy-start.29 = (f32[512]{0:T(512)S(1)}, f32[512]{0:T(512)}, u32[]{:S(2)}) copy-start(f32[512]{0:T(512)} %copy-done.28) | copy-start | bytes 6148
  730.1 181.0 %reduce-scatter.13.cloned.1.call-start = ((), (), s32[]{:S(2)}) async-start(), calls=%async_computation.19 | async-start | bytes 2359296 | tf_op jit(solution)/shard_map/reduce_scatter | solution.py:230
  740.9 20.7 %copy-start.3 = (f32[512,1024]{1,0:T(8,128)S(1)}, f32[512,1024]{1,0:T(8,128)}, u32[]{:S(2)}) copy-start(f32[512,1024]{1,0:T(8,128)} %copy-done.2) | copy-start | bytes 6291460
  779.8 196.7 %reduce-scatter.11.cloned.1.call-start = ((), (), s32[]{:S(2)}) async-start(), calls=%async_computation.18 | async-start | bytes 7077888 | tf_op jit(solution)/shard_map/reduce_scatter | solution.py:227
  791.6 13.2 %copy-start.4 = (bf16[512,3072]{0,1:T(8,128)(2,1)S(1)}, bf16[512,3072]{0,1:T(8,128)(2,1)}, u32[]{:S(2)}) copy-start(bf16[512,3072]{0,1:T(8,128)(2,1)} %copy.47) | copy-start | bytes 9437188
  826.1 276.0 %all-reduce.4.cloned.1.call-start = ((), (), s32[]{:S(2)}) async-start(), calls=%async_computation.22 | async-start | bytes 6291456 | tf_op jit(solution)/shard_map/psum | solution.py:241
  976.5 11.6 %copy-start.17 = (bf16[512,3,16,64]{0,3,2,1:T(8,128)(2,1)S(1)}, bf16[512,3,16,64]{0,3,2,1:T(8,128)(2,1)}, u32[]{:S(2)}) copy-start(bf16[512,3,16,64]{0,3,2,1:T(8,128)(2,1)} %copy-done.16) | copy-start | bytes 9437188
  988.1 51.2 %copy-start.15 = (bf16[512,1024]{1,0:T(8,128)(2,1)S(1)}, bf16[512,1024]{1,0:T(8,128)(2,1)}, u32[]{:S(2)}) copy-start(bf16[512,1024]{1,0:T(8,128)(2,1)} %param.25) | copy-start | bytes 3145732
  (26 other events, 76.5 us)
Sparse Core Ops, SparseCore 0:
  9.9 48.2 all-gather.6
  60.1 27.8 all-gather.8
  126.6 97.1 all-gather.14
  244.8 92.1 reduce-scatter.6
  338.7 64.6 all-gather.10
  405.1 53.9 all-gather.12
  494.9 97.1 all-gather.16
  617.3 92.1 reduce-scatter.8
  712.9 78.0 reduce-scatter.16
  794.7 71.2 reduce-scatter.14
  869.9 41.1 reduce-scatter.12
  914.7 61.7 reduce-scatter.10
  979.1 123.0 all-reduce.3
where the time goes:
time: 1120 us
  waiting for transfers between devices  673 us (60%)
  matrix products  214 us (19%)
  blocking collectives  85.4 us (8%)
  other arithmetic  67 us (6%)
  local copies, waits for them, and re-layouts  52 us (5%)
  between operations  15.4 us (1%)
    all_gather x1, waiting for transfers between devices, on_device(): slot_rows = lax.all_gather(arrived, 'dp', axis=1, tiled=True)  97.3 us
    all_gather x1, waiting for transfers between devices, on_device(): slot_grad = lax.all_gather(arrived_grad, 'dp', axis=1, tiled=True)  97 us
    reduce_scatter x1, waiting for transfers between devices, on_device(): lax.psum_scatter(partial_out.astype(jnp.bfloat16), 'dp', scatter_dimensio...  90.7 us
    reduce_scatter x1, waiting for transfers between devices, on_device(): lax.psum_scatter(qkv_weight_grad.astype(jnp.bfloat16), 'ep', scatter_dime...  65.4 us
    psum x1, waiting for transfers between devices, on_device(): lax.psum(batch_sums[0].astype(jnp.bfloat16), 'dp').astype(jnp.float32)  58.4 us
    reduce_scatter x1, waiting for transfers between devices, on_device(): lax.psum_scatter(partial_in.astype(jnp.bfloat16), 'dp', scatter_dimension...  56.6 us
    reduce_scatter x1, waiting for transfers between devices, on_device(): lax.psum_scatter(out_weight_grad.astype(jnp.bfloat16), 'ep', scatter_dime...  45.1 us
    psum x1, blocking collectives, on_device(): lax.psum((ln1_gain_grad, ln2_gain_grad, mix_weight_grad), ('dp', 'ep'))  42.8 us
  transfers between devices with their start and end apart: 15, of which 12 were waited for; matrix products, arithmetic and copies ran while one was open for 22% of the time, Pallas kernels for 0%

commit v1 on v0

--- a/solution.py
+++ b/solution.py
@@ -238,7 +238,9 @@
         ).astype(jnp.float32),
     )
     dense_shards = (
-        lax.psum(batch_sums[0].astype(jnp.bfloat16), "dp").astype(jnp.float32),
+        jnp.sum(lax.all_gather(batch_sums[0].astype(jnp.bfloat16), "dp"), axis=0).astype(
+            jnp.float32
+        ),
         lax.psum(batch_sums[1].astype(jnp.bfloat16), "dp").astype(jnp.float32),
         lax.psum(batch_sums[2].astype(jnp.bfloat16), "dp").astype(jnp.float32),
         lax.psum(batch_sums[3].astype(jnp.bfloat16), "dp").astype(jnp.float32),

time: 1120 us -> 1150 us (1.027)
  waiting for transfers between devices: 673 us -> 707 us
    all_gather x0 -> x1, waiting for transfers between devices: none -> 57.7 us  [on_device(): lax.all_gather(batch_sums[0].astype(jnp.bfloat16), 'dp')]
    psum x1, waiting for transfers between devices: 58.4 us -> 23.9 us  [on_device(): lax.psum(batch_sums[1].astype(jnp.bfloat16), 'dp').astype(jnp.float32)]
  transfers between devices with their start and end apart: 15 -> 16, of which waited for: 12 -> 13; matrix products, arithmetic and copies ran while one was open for 22% -> 22% of each run, Pallas kernels for 0% -> 0%
where the time goes in v1:
time: 1150 us
  waiting for transfers between devices  707 us (61%)
  matrix products  214 us (19%)
  blocking collectives  82.9 us (7%)
  other arithmetic  68.3 us (6%)
  local copies, waits for them, and re-layouts  52 us (5%)
  between operations  15.4 us (1%)
    all_gather x1, waiting for transfers between devices, on_device(): slot_rows = lax.all_gather(arrived, 'dp', axis=1, tiled=True)  97.3 us
    all_gather x1, waiting for transfers between devices, on_device(): slot_grad = lax.all_gather(arrived_grad, 'dp', axis=1, tiled=True)  97 us
    reduce_scatter x1, waiting for transfers between devices, on_device(): lax.psum_scatter(partial_out.astype(jnp.bfloat16), 'dp', scatter_dimensio...  90.7 us
    reduce_scatter x1, waiting for transfers between devices, on_device(): lax.psum_scatter(qkv_weight_grad.astype(jnp.bfloat16), 'ep', scatter_dime...  64.8 us
    all_gather x1, waiting for transfers between devices, on_device(): lax.all_gather(batch_sums[0].astype(jnp.bfloat16), 'dp')  57.7 us
    reduce_scatter x1, waiting for transfers between devices, on_device(): lax.psum_scatter(partial_in.astype(jnp.bfloat16), 'dp', scatter_dimension...  56.6 us
    reduce_scatter x1, waiting for transfers between devices, on_device(): lax.psum_scatter(out_weight_grad.astype(jnp.bfloat16), 'ep', scatter_dime...  45.1 us
    all_gather x1, waiting for transfers between devices, on_device(): lax.all_gather(up_weight, 'ep', axis=0, tiled=True)  41.4 us
  transfers between devices with their start and end apart: 16, of which 13 were waited for; matrix products, arithmetic and copies ran while one was open for 22% of the time, Pallas kernels for 0%

profile of v1, /device:TPU:0, one launch (start us, length us, event | category | flops | bytes accessed | tf_op | source)
XLA Modules:
  0.0 1150.2 jit_solution(11915806450656047086)
XLA Ops:
  17.8 40.4 %all-gather.9.cloned.1.call-done = bf16[1024,3072]{1,0:T(8,128)(2,1)} async-done(((bf16[128,3072]{1,0:T(8,128)(2,1)}), bf16[1024,3072]{1,0:T(8,128)(2,1)}) %all-gather.9.cloned.1.call-update) | async-done | bytes 6291472 | tf_op jit(solution)/shard_map/all_gather | solution.py:103
  70.8 10.1 fusion.99
  89.3 10.1 fusion.56
  105.2 21.3 %all_to_all.42 = bf16[8,80,1024]{2,1,0:T(8,128)(2,1)} all-to-all(bf16[8,80,1024]{2,1,0:T(8,128)(2,1)S(1)} %bitcast.158), channel_id=1, replica_groups=mesh['dp'=4,'ep'=8] {'ep'}, dimensions={0} | all-to-all | bytes 2621440 | tf_op jit(solution)/shard_map/all_to_all | solution.py:136
  126.5 97.3 %all-gather.17.cloned.1.call-done = bf16[1,2560,1024]{2,1,0:T(8,128)(2,1)} async-done(((bf16[1,640,1024]{2,1,0:T(8,128)(2,1)}), bf16[1,2560,1024]{2,1,0:T(8,128)(2,1)}) %all-gather.17.cloned.1.call-update) | async-done | bytes 5242896 | tf_op jit(solution)/shard_map/all_gather | solution.py:139
  223.8 8.6 fusion.28
  246.3 90.7 %reduce-scatter.7.cloned.1.call-done = bf16[1,640,1024]{2,1,0:T(8,128)(2,1)} async-done(((bf16[1,2560,1024]{2,1,0:T(8,128)(2,1)}), bf16[1,640,1024]{2,1,0:T(8,128)(2,1)}) %reduce-scatter.7.cloned.1.call-update) | async-done | bytes 1310736 | tf_op jit(solution)/shard_map/reduce_scatter | solution.py:147
  342.3 10.7 reduce.3
  361.9 41.4 %all-gather.13.cloned.1.call-done = bf16[1024,4096]{1,0:T(8,128)(2,1)} async-done(((bf16[128,4096]{1,0:T(8,128)(2,1)}), bf16[1024,4096]{1,0:T(8,128)(2,1)}) %all-gather.13.cloned.1.call-update) | async-done | bytes 8388624 | tf_op jit(solution)/shard_map/all_gather | solution.py:105
  403.4 10.0 fusion.104
  423.9 35.3 %all-gather.15.cloned.1.call-done = bf16[4096,1024]{1,0:T(8,128)(2,1)} async-done(((bf16[512,1024]{1,0:T(8,128)(2,1)}), bf16[4096,1024]{1,0:T(8,128)(2,1)}) %all-gather.15.cloned.1.call-update) | async-done | bytes 8388624 | tf_op jit(solution)/shard_map/all_gather | solution.py:106
  459.1 13.3 %fusion.49 = (f32[512]{0:T(512)S(1)}, f32[512]{0:T(512)S(1)}, f32[512,1024]{1,0:T(8,128)}) fusion(bf16[512,1024]{1,0:T(8,128)(2,1)} %param.25, f32[512,1024]{1,0:T(8,128)} %fusion.68, bf16[4096,1024]{1,0:T(8,128)(2,1)} %all-gather.15.cloned.1.call-done, f32[512,4096]{1,0:T(8,128)} %fusion.104), kind=kOutput, calls=%fused_computation.71 | convolution fusion | flops 4316462080 | bytes 22024192 | tf_op jit(solution)/shard_map/dot_general | solution.py:122
  473.5 21.3 %all_to_all.43 = bf16[8,80,1024]{2,1,0:T(8,128)(2,1)} all-to-all(bf16[8,80,1024]{2,1,0:T(8,128)(2,1)S(1)} %bitcast.159), channel_id=1, replica_groups=mesh['dp'=4,'ep'=8] {'ep'}, dimensions={0} | all-to-all | bytes 2621440 | tf_op jit(solution)/shard_map/all_to_all | solution.py:184
  495.1 97.0 %all-gather.19.cloned.1.call-done = bf16[1,2560,1024]{2,1,0:T(8,128)(2,1)} async-done(((bf16[1,640,1024]{2,1,0:T(8,128)(2,1)}), bf16[1,2560,1024]{2,1,0:T(8,128)(2,1)}) %all-gather.19.cloned.1.call-update) | async-done | bytes 5242896 | tf_op jit(solution)/shard_map/all_gather | solution.py:187
  592.1 14.9 %fusion.8 = bf16[2560,1024]{1,0:T(8,128)(2,1)S(1)} fusion(f32[2560,1024]{1,0:T(8,128)} %copy-done.41, bf16[1,2560,1024]{2,1,0:T(8,128)(2,1)} %all-gather.19.cloned.1.call-done, bf16[1,1024,1024]{2,1,0:T(8,128)(2,1)S(1)} %copy-done), kind=kOutput, calls=%fused_computation.18 | convolution fusion | flops 5421137920 | bytes 23068672 | tf_op jit(solution)/shard_map/erd,efd->erf/dot_general | solution.py:188
  618.4 10.3 convolution_convert_fusion
  629.0 12.5 %fusion.15 = bf16[512,4096]{1,0:T(8,128)(2,1)S(1)} fusion(f32[512,4096]{1,0:T(8,128)} %fusion.104, bf16[4096,1024]{1,0:T(8,128)(2,1)} %all-gather.15.cloned.1.call-done, bf16[512,1024]{1,0:T(8,128)(2,1)S(1)} %copy-done.13, f32[512]{0:T(512)S(1)} %bitcast.172), kind=kOutput, calls=%fused_computation.26 | convolution fusion | flops 4338483200 | bytes 22022144 | tf_op jit(solution)/shard_map/td,fd->tf/dot_general | solution.py:169
  652.9 56.6 %reduce-scatter.9.cloned.1.call-done = bf16[1,640,1024]{2,1,0:T(8,128)(2,1)} async-done(((bf16[1,2560,1024]{2,1,0:T(8,128)(2,1)}), bf16[1,640,1024]{2,1,0:T(8,128)(2,1)}) %reduce-scatter.9.cloned.1.call-update) | async-done | bytes 1310736 | tf_op jit(solution)/shard_map/reduce_scatter | solution.py:201
  714.4 9.6 reduce.4
  730.3 10.6 fusion.105
  740.9 14.5 %all-to-all-done.3 = bf16[8,2,40960]{2,1,0:T(2,128)(2,1)} async-done(((bf16[8,2,40960]{2,1,0:T(2,128)(2,1)}), bf16[8,2,40960]{2,1,0:T(2,128)(2,1)}, u32[]{:S(2)}, u32[]{:S(2)}) %all-to-all-start.3) | async-done | bytes 1310752 | tf_op jit(solution)/shard_map/all_to_all | solution.py:204
  780.1 11.5 %multiply_reduce_fusion = (f32[16,512]{1,0:T(8,128)S(1)}, f32[16,512,512]{1,2,0:T(8,128)}) fusion(f32[16,512,512]{1,2,0:T(8,128)} %get-tuple-element.31, f32[16,512]{1,0:T(8,128)S(1)} %log_add_fusion, bf16[512,16,64]{0,2,1:T(8,128)(2,1)S(1)} %bitcast.145, bf16[512,3,16,64]{0,3,2,1:T(8,128)(2,1)} %bitcast.140), kind=kOutput, calls=%fused_computation.1 | convolution fusion | flops 549445632 | bytes 35717120 | tf_op jit(solution)/shard_map/qhd,khd->hqk/dot_general | solution.py:60
  791.6 12.9 %multiply_convert_fusion = bf16[16,512,512]{1,2,0:T(8,128)(2,1)S(1)} fusion(f32[16,512,512]{1,2,0:T(8,128)} %get-tuple-element.39, f32[16,512,512]{1,2,0:T(8,128)} %get-tuple-element.31, f32[16,512]{1,0:T(8,128)S(1)} %get-tuple-element.38, f32[16,512]{1,0:T(8,128)S(1)} %log_add_fusion), kind=kLoop, calls=%fused_computation | loop fusion | flops 16777216 | bytes 42008576 | tf_op jit(solution)/shard_map/convert_element_type | solution.py:64
  809.0 9.0 fusion.62
  826.2 39.8 %reduce-scatter.15.cloned.1.call-done = bf16[128,4096]{1,0:T(8,128)(2,1)} async-done(((bf16[1024,4096]{1,0:T(8,128)(2,1)}), bf16[128,4096]{1,0:T(8,128)(2,1)}) %reduce-scatter.15.cloned.1.call-update) | async-done | bytes 1048592 | tf_op jit(solution)/shard_map/reduce_scatter | solution.py:233
  866.0 45.1 %reduce-scatter.13.cloned.1.call-done = bf16[128,1024]{1,0:T(8,128)(2,1)} async-done(((bf16[1024,1024]{1,0:T(8,128)(2,1)}), bf16[128,1024]{1,0:T(8,128)(2,1)}) %reduce-scatter.13.cloned.1.call-update) | async-done | bytes 262160 | tf_op jit(solution)/shard_map/reduce_scatter | solution.py:230
  911.7 64.8 %reduce-scatter.11.cloned.1.call-done = bf16[128,3072]{1,0:T(8,128)(2,1)} async-done(((bf16[1024,3072]{1,0:T(8,128)(2,1)}), bf16[128,3072]{1,0:T(8,128)(2,1)}) %reduce-scatter.11.cloned.1.call-update) | async-done | bytes 786448 | tf_op jit(solution)/shard_map/reduce_scatter | solution.py:227
  976.5 11.4 fusion.38
  988.0 10.6 fusion.41
  1006.9 40.3 %all-reduce = (f32[1024]{0:T(1024)}, f32[1024]{0:T(1024)}, f32[1024,2]{0,1:T(2,128)}) all-reduce(f32[1024]{0:T(1024)S(1)} %get-tuple-element.13, f32[1024]{0:T(1024)S(1)} %get-tuple-element.11, f32[1024,2]{0,1:T(2,128)S(1)} %fusion.102), channel_id=1, replica_groups=mesh['dp'=4,'ep'=8] {'dp','ep'}, use_global_device_ids=true, to_apply=%region_22.23 | all-reduce | flops 4096 | bytes 32768 | tf_op jit(solution)/shard_map/psum | solution.py:248
  1051.7 23.9 %all-reduce.4.cloned.1.call-done = (bf16[128,1024]{1,0:T(8,128)(2,1)}, bf16[128,4096]{1,0:T(8,128)(2,1)}, bf16[512,1024]{1,0:T(8,128)(2,1)}) async-done(((bf16[128,1024]{1,0:T(8,128)(2,1)}, bf16[128,4096]{1,0:T(8,128)(2,1)}, bf16[512,1024]{1,0:T(8,128)(2,1)}), (bf16[128,1024]{1,0:T(8,128)(2,1)}, bf16[128,4096]{1,0:T(8,128)(2,1)}, bf16[512,1024]{1,0:T(8,128)(2,1)})) %all-reduce.4.cloned.1.call-update) | async-done | bytes 2359312 | tf_op jit(solution)/shard_map/psum | solution.py:244
  1081.9 57.7 %all-gather.21.cloned.1.call-done = bf16[512,3072]{1,0:T(8,128)(2,1)} async-done(((bf16[128,3072]{1,0:T(8,128)(2,1)}), bf16[512,3072]{1,0:T(8,128)(2,1)}) %all-gather.21.cloned.1.call-update) | async-done | bytes 3145744 | tf_op jit(solution)/shard_map/all_gather | solution.py:241
  (184 shorter events, 171.2 us)
Async XLA Ops:
  7.2 229.2 %copy-start = (bf16[1,1024,1024]{2,1,0:T(8,128)(2,1)S(1)}, bf16[1,1024,1024]{2,1,0:T(8,128)(2,1)}, u32[]{:S(2)}) copy-start(bf16[1,1024,1024]{2,1,0:T(8,128)(2,1)} %param.24) | copy-start | bytes 6291460
  7.2 51.0 %copy-start.5 = (bf16[512,1024]{1,0:T(8,128)(2,1)S(1)}, bf16[512,1024]{1,0:T(8,128)(2,1)}, u32[]{:S(2)}) copy-start(bf16[512,1024]{1,0:T(8,128)(2,1)} %param.13) | copy-start | bytes 3145732
  7.2 51.0 %copy-start.36 = (f32[1024]{0:T(1024)S(1)}, f32[1024]{0:T(1024)}, u32[]{:S(2)}) copy-start(f32[1024]{0:T(1024)} %param.16) | copy-start | bytes 12292
  7.2 51.0 %all-gather.9.cloned.1.call-start = ((), (), s32[]{:S(2)}) async-start(), calls=%async_computation.10 | async-start | bytes 7077888 | tf_op jit(solution)/shard_map/all_gather | solution.py:103
  8.0 91.4 %all-gather.11.cloned.1.call-start = ((), (), s32[]{:S(2)}) async-start(), calls=%async_computation.11 | async-start | bytes 2359296 | tf_op jit(solution)/shard_map/all_gather | solution.py:104
  8.7 215.1 %all-gather.17.cloned.1.call-start = ((), (), s32[]{:S(2)}) async-start(), calls=%async_computation.14 | async-start | bytes 6553600 | tf_op jit(solution)/shard_map/all_gather | solution.py:139
  10.9 55.1 %copy-start.26 = (f32[512]{0:T(512)}, f32[512]{0:T(512)S(1)}, u32[]{:S(2)}) copy-start(f32[512]{0:T(512)S(1)} %broadcast_multiply_fusion.1) | copy-start | bytes 6148
  12.5 53.4 %copy-start.30 = (f32[512]{0:T(512)}, f32[512]{0:T(512)S(1)}, u32[]{:S(2)}) copy-start(f32[512]{0:T(512)S(1)} %fusion.90) | copy-start | bytes 6148
  103.1 23.4 %copy-start.34 = (f32[512]{0:T(512)}, f32[512]{0:T(512)S(1)}, u32[]{:S(2)}) copy-start(f32[512]{0:T(512)S(1)} %multiply_reduce_fusion.3) | copy-start | bytes 6148
  103.1 23.4 %copy-start.28 = (f32[512]{0:T(512)}, f32[512]{0:T(512)S(1)}, u32[]{:S(2)}) copy-start(f32[512]{0:T(512)S(1)} %fusion.91) | copy-start | bytes 6148
  126.5 210.5 %reduce-scatter.7.cloned.1.call-start = ((), (), s32[]{:S(2)}) async-start(), calls=%async_computation.15 | async-start | bytes 6553600 | tf_op jit(solution)/shard_map/reduce_scatter | solution.py:147
  244.7 158.7 %all-gather.13.cloned.1.call-start = ((), (), s32[]{:S(2)}) async-start(), calls=%async_computation.12 | async-start | bytes 9437184 | tf_op jit(solution)/shard_map/all_gather | solution.py:105
  245.3 213.9 %all-gather.15.cloned.1.call-start = ((), (), s32[]{:S(2)}) async-start(), calls=%async_computation.13 | async-start | bytes 9437184 | tf_op jit(solution)/shard_map/all_gather | solution.py:106
  357.4 56.0 %all-to-all-start.1 = ((bf16[8,2,40960]{2,1,0:T(2,128)(2,1)}), bf16[8,2,40960]{2,1,0:T(2,128)(2,1)}, u32[]{:S(2)}, u32[]{:S(2)}) async-start(bf16[8,2,40960]{2,1,0:T(2,128)(2,1)} %reshape.350), calls=%async_computation.2 | async-start | bytes 2621440 | tf_op jit(solution)/shard_map/all_to_all | solution.py:150
  361.7 230.4 %all-gather.19.cloned.1.call-start = ((), (), s32[]{:S(2)}) async-start(), calls=%async_computation.16 | async-start | bytes 6553600 | tf_op jit(solution)/shard_map/all_gather | solution.py:187
  459.1 13.4 %copy-start.11 = (bf16[512,8,80]{0,2,1:T(8,128)(2,1)S(1)}, bf16[512,8,80]{0,2,1:T(8,128)(2,1)}, u32[]{:S(2)}) copy-start(bf16[512,8,80]{0,2,1:T(8,128)(2,1)} %multiply_convert_fusion.6) | copy-start | bytes 1966084
  459.1 13.4 %copy-start.12 = (bf16[512,1024]{1,0:T(8,128)(2,1)S(1)}, bf16[512,1024]{1,0:T(8,128)(2,1)}, u32[]{:S(2)}) copy-start(bf16[512,1024]{1,0:T(8,128)(2,1)} %param.25) | copy-start | bytes 3145732
  494.8 214.6 %reduce-scatter.9.cloned.1.call-start = ((), (), s32[]{:S(2)}) async-start(), calls=%async_computation.17 | async-start | bytes 6553600 | tf_op jit(solution)/shard_map/reduce_scatter | solution.py:201
  592.1 17.3 %copy-start.39 = (bf16[1,1024,1024]{2,1,0:T(8,128)(2,1)S(1)}, bf16[1,1024,1024]{2,1,0:T(8,128)(2,1)}, u32[]{:S(2)}) copy-start(bf16[1,1024,1024]{2,1,0:T(8,128)(2,1)} %param.23) | copy-start | bytes 6291460
  617.2 209.1 %reduce-scatter.17.cloned.1.call-start = ((), (), s32[]{:S(2)}) async-start(), calls=%async_computation.21 | async-start | bytes 9437184 | tf_op jit(solution)/shard_map/reduce_scatter | solution.py:236
  628.7 237.3 %reduce-scatter.15.cloned.1.call-start = ((), (), s32[]{:S(2)}) async-start(), calls=%async_computation.20 | async-start | bytes 9437184 | tf_op jit(solution)/shard_map/reduce_scatter | solution.py:233
  725.8 29.6 %all-to-all-start.3 = ((bf16[8,2,40960]{2,1,0:T(2,128)(2,1)}), bf16[8,2,40960]{2,1,0:T(2,128)(2,1)}, u32[]{:S(2)}, u32[]{:S(2)}) async-start(bf16[8,2,40960]{2,1,0:T(2,128)(2,1)} %reshape.352), calls=%async_computation.5 | async-start | bytes 2621440 | tf_op jit(solution)/shard_map/all_to_all | solution.py:204
  730.1 31.5 %copy-start.23 = (f32[512]{0:T(512)S(1)}, f32[512]{0:T(512)}, u32[]{:S(2)}) copy-start(f32[512]{0:T(512)} %copy-done.22) | copy-start | bytes 6148
  730.1 31.5 %copy-start.25 = (f32[1024]{0:T(1024)S(1)}, f32[1024]{0:T(1024)}, u32[]{:S(2)}) copy-start(f32[1024]{0:T(1024)} %param.19) | copy-start | bytes 12292
  730.1 31.5 %copy-start.29 = (f32[512]{0:T(512)S(1)}, f32[512]{0:T(512)}, u32[]{:S(2)}) copy-start(f32[512]{0:T(512)} %copy-done.28) | copy-start | bytes 6148
  730.1 181.0 %reduce-scatter.13.cloned.1.call-start = ((), (), s32[]{:S(2)}) async-start(), calls=%async_computation.19 | async-start | bytes 2359296 | tf_op jit(solution)/shard_map/reduce_scatter | solution.py:230
  740.9 20.7 %copy-start.3 = (f32[512,1024]{1,0:T(8,128)S(1)}, f32[512,1024]{1,0:T(8,128)}, u32[]{:S(2)}) copy-start(f32[512,1024]{1,0:T(8,128)} %copy-done.2) | copy-start | bytes 6291460
  779.8 196.7 %reduce-scatter.11.cloned.1.call-start = ((), (), s32[]{:S(2)}) async-start(), calls=%async_computation.18 | async-start | bytes 7077888 | tf_op jit(solution)/shard_map/reduce_scatter | solution.py:227
  826.1 249.5 %all-reduce.4.cloned.1.call-start = ((), (), s32[]{:S(2)}) async-start(), calls=%async_computation.23 | async-start | bytes 4718592 | tf_op jit(solution)/shard_map/psum | solution.py:244
  911.1 228.4 %all-gather.21.cloned.1.call-start = ((), (), s32[]{:S(2)}) async-start(), calls=%async_computation.22 | async-start | bytes 3932160 | tf_op jit(solution)/shard_map/all_gather | solution.py:241
  998.5 48.7 %copy-start.15 = (bf16[512,1024]{1,0:T(8,128)(2,1)S(1)}, bf16[512,1024]{1,0:T(8,128)(2,1)}, u32[]{:S(2)}) copy-start(bf16[512,1024]{1,0:T(8,128)(2,1)} %param.25) | copy-start | bytes 3145732
  1080.3 63.1 %copy-start.1 = (bf16[1,1024,1024]{2,1,0:T(8,128)(2,1)S(1)}, bf16[1,1024,1024]{2,1,0:T(8,128)(2,1)}, u32[]{:S(2)}) copy-start(bf16[1,1024,1024]{2,1,0:T(8,128)(2,1)} %param.24) | copy-start | bytes 6291460
  (27 other events, 90.8 us)
Sparse Core Ops, SparseCore 0:
  9.9 48.2 all-gather.8
  60.1 27.8 all-gather.10
  126.6 97.1 all-gather.16
  244.8 92.1 reduce-scatter.6
  338.7 64.6 all-gather.12
  405.1 53.9 all-gather.14
  494.9 97.1 all-gather.18
  617.3 92.1 reduce-scatter.8
  712.9 78.0 reduce-scatter.16
  794.7 71.2 reduce-scatter.14
  869.9 41.1 reduce-scatter.12
  914.7 61.7 reduce-scatter.10
  979.1 96.5 all-reduce.3
  1077.1 62.4 all-gather.20
